TPU v7x, 32 devices: a whole 2x2x4 slice. The times are simulated.
32 devices in a mesh: seq: 8 (over y, x, core), head: 4 (over z).
Axes of the slice: x: 2, y: 2, z: 4, core: 2. Of those that a mesh axis runs over, the one named last changes fastest.
Arguments:
- ssm_input: bfloat16 [1536, 16384], P('seq', 'head'), may hold values from -6 to 6
- state_in: bfloat16 [1536, 2048], P('seq'), may hold values from -0.375 to 0.375
- state_out: bfloat16 [1536, 2048], P('seq'), may hold values from -0.15625 to 0.15625
- step_size: float32 [1536, 256], P('seq', 'head'), may hold values from 0.5 to 1.5
- decay_rate: float32 [256], P('head'), may hold values from 3.25520833e-05 to 0.04
- forget: float32 [1536], P('seq'), may hold values from 0 to 0.9
- skip_gain: float32 [256], P('head'), may hold values from 0.25 to 1.75
- queries: bfloat16 [1536, 8192], P('seq', 'head'), may hold values from -48 to 48
- new_keys: bfloat16 [1536, 1024], P('seq'), may hold values from -6 to 6
- new_values: bfloat16 [1536, 1024], P('seq'), may hold values from -6 to 6
- cache_keys: bfloat16 [1024, 1024], P('seq'), may hold values from -127 to 127, as said below
- cache_values: bfloat16 [1024, 1024], P('seq'), may hold values from -127 to 127, as said below
- cache_key_scale: float32 [1024], replicated, may hold values from 0.003 to 0.03
- cache_value_scale: float32 [1024], replicated, may hold values from 0.003 to 0.03
Outputs:
- ssm_output: bfloat16 [1536, 16384], P('seq', 'head')
- attended: bfloat16 [1536, 8192], P('seq', 'head')
- key_codes: bfloat16 [1536, 1024], P('seq')
- key_scale: float32 [1024], replicated
Inputs may be any that keep to these rules, and one draw needn't show every extreme that they name: `cache_keys`: whole numbers. `cache_values`: whole numbers.
All inputs are finite; a program needn't handle non-finite values.
Results may differ from a plain program's by a relative error of at most 0.019.
Values may be sent and summed in bfloat16 or wider, within the bound.
A program may use at most 128 MiB of HBM per device.

v0:
```python
import functools
import jax
import jax.numpy as jnp
from jax import lax
from jax.experimental import pallas as pl
from jax.experimental.pallas import tpu as pltpu
from jax.sharding import PartitionSpec as P

SSM_HEADS = 256
HEAD_DIM = 64
STATE = 256
GROUPS = 8
ATT_HEADS = 64
KV_HEADS = 8
ATT_DIM = 128

NEG = -1e30
LOG2E = 1.4426950408889634
HIGHEST = lax.Precision.HIGHEST
MESH = pl.DeviceIdType.MESH
VMEM = pl.BlockSpec(memory_space=pltpu.VMEM)
F32 = jnp.float32
BF16 = jnp.bfloat16


def iota(shape, axis):
    return lax.broadcasted_iota(jnp.int32, shape, axis)


def lanes(start, size):
    return pl.ds(pl.multiple_of(start, 128), size)


def local_kernel(
    x_ref,
    sin_ref,
    sout_ref,
    step_ref,
    decay_ref,
    forget_ref,
    skip_ref,
    nk_ref,
    nv_ref,
    ck_ref,
    cv_ref,
    cks_ref,
    cvs_ref,
    state_ref,
    part_ref,
    fade_ref,
    meta_ref,
    kvc_ref,
    kvn_ref,
    gram_ref,
    bt_ref,
    at_ref,
):
    tokens, width = x_ref.shape
    heads = step_ref.shape[1]
    per_group = min(SSM_HEADS // GROUPS, heads)
    groups_here = heads // per_group
    z = lax.axis_index("head")
    group0 = z * heads // (SSM_HEADS // GROUPS)
    kvw = kvc_ref.shape[1] // 2
    q_heads = heads * ATT_HEADS // SSM_HEADS
    first = z * q_heads // (ATT_HEADS // KV_HEADS)
    cols = lanes(first * ATT_DIM, kvw)
    kvc_ref[:, :kvw] = (ck_ref[:, cols].astype(F32) * cks_ref[:, cols]).astype(BF16)
    kvc_ref[:, kvw:] = (cv_ref[:, cols].astype(F32) * cvs_ref[:, cols]).astype(BF16)
    kvn_ref[:, :kvw] = nk_ref[:, cols]
    kvn_ref[:, kvw:] = nv_ref[:, cols]
    meta_ref[:, width:] = jnp.max(jnp.abs(nk_ref[...].astype(F32)), axis=0, keepdims=True)

    rate = (-decay_ref[...] * step_ref[...] - forget_ref[...]) * LOG2E
    row, col = iota((tokens, tokens), 0), iota((tokens, tokens), 1)
    lower = jnp.where(col <= row, 1.0, 0.0)
    eye = jnp.where(col == row, 1.0, 0.0)
    running = jnp.dot(lower, rate, precision=HIGHEST, preferred_element_type=F32)
    lstep = jnp.log2(step_ref[...])
    start = running - lstep
    at_ref[...] = lax.dot_general(
        start, eye, (((0,), (0,)), ((), ())), precision=HIGHEST, preferred_element_type=F32
    )
    tail = jnp.exp2(running[tokens - 1 : tokens] - start).astype(BF16)
    for g in range(groups_here):
        gcols = lanes((group0 + g) * STATE, STATE)
        maps_in = sin_ref[:, gcols]
        gram_ref[g] = lax.dot_general(
            sout_ref[:, gcols], maps_in, (((1,), (1,)), ((), ())), preferred_element_type=F32
        )
        bt_ref[g] = lax.dot_general(
            maps_in,
            eye.astype(BF16),
            (((0,), (0,)), ((), ())),
            preferred_element_type=F32,
        ).astype(BF16)

    def pair(p, _):
        here = lanes(p * 128, 128)
        g = (2 * p) // per_group
        pick = (iota((heads, 128), 0) == 2 * p + iota((heads, 128), 1) // HEAD_DIM).astype(F32)
        run = jnp.dot(running, pick, precision=HIGHEST, preferred_element_type=F32)
        meta_ref[:, here] = run[tokens - 1 : tokens]
        fade_ref[:, here] = jnp.exp2(run).astype(BF16)
        x = x_ref[:, here]
        scale = jnp.dot(tail, pick.astype(BF16), preferred_element_type=F32)
        scaled = (x.astype(F32) * scale).astype(BF16)
        state_ref[:, here] = jnp.dot(
            bt_ref[g], scaled, preferred_element_type=F32
        ).astype(BF16)
        gram = gram_ref[g]
        causal = iota((tokens, tokens), 1) <= iota((tokens, tokens), 0)

        def one(k):
            spread = run[:, k * HEAD_DIM : k * HEAD_DIM + 1] - at_ref[pl.ds(2 * p + k, 1), :]
            weight = jnp.exp2(jnp.where(causal, spread, NEG)) * gram
            return jnp.dot(weight.astype(BF16), x, preferred_element_type=F32)

        y = jnp.where(iota((tokens, 128), 1) < HEAD_DIM, one(0), one(1))
        part_ref[:, here] = (y + skip_ref[:, here] * x.astype(F32)).astype(BF16)
        return 0

    lax.fori_loop(0, heads // 2, pair, 0)


def comm_kernel(
    n,
    chunks,
    state_ref,
    kvc_ref,
    kvn_ref,
    meta_ref,
    out_ref,
    allc_ref,
    alln_ref,
    allm_ref,
    sib_ref,
    own_ref,
    incl_ref,
    recv_ref,
    back_ref,
    meta_s,
    meta_r,
    kv_s,
    kv_r,
    kv_f,
    sib_s,
    sib_r,
    pre_s,
    pre_r,
    rel_s,
    back_s,
    back_r,
):
    n2 = n // 2
    levels = n2.bit_length() - 1
    me = lax.axis_index("seq")
    i, c = me % 2, me // 2
    other = me + 1 - 2 * i
    width = state_ref.shape[1]
    half = width // 2
    size = half // chunks

    barrier = pltpu.get_barrier_semaphore()
    for d in range(1, n):
        pl.semaphore_signal(
            barrier, inc=1, device_id={"seq": (me + d) % n}, device_id_type=MESH
        )
    pl.semaphore_wait(barrier, n - 1)

    def remote(src, dst, ssem, rsem, to):
        return pltpu.make_async_remote_copy(
            src_ref=src,
            dst_ref=dst,
            send_sem=ssem,
            recv_sem=rsem,
            device_id={"seq": to},
            device_id_type=MESH,
        )

    def sib_copy(j):
        return remote(
            state_ref.at[:, lanes((1 - i) * half + j * size, size)],
            sib_ref.at[j],
            sib_s.at[j],
            sib_r.at[j],
            other,
        )

    for j in range(chunks):
        sib_copy(j).start()
    for d in range(1, n):
        remote(
            meta_ref, allm_ref.at[me], meta_s.at[d], meta_r.at[me], (me + d) % n
        ).start()

    def cache_copy(d, to):
        return remote(kvc_ref, allc_ref.at[me], kv_s.at[0, d], kv_r.at[0, me], to)

    def new_copy(d, to):
        return remote(kvn_ref, alln_ref.at[me], kv_s.at[1, d], kv_r.at[1, me], to)

    cache_copy(0, other).start()
    new_copy(0, other).start()
    for d in range(1, n2):
        to = ((c + d) % n2) * 2 + i
        cache_copy(d, to).start()

        @pl.when(c + d < n2)
        def _():
            new_copy(d, to).start()

    allm_ref[me] = meta_ref[...]
    allc_ref[me] = kvc_ref[...]
    alln_ref[me] = kvn_ref[...]
    for d in range(1, n2):
        later = c + d

        @pl.when(later < n2)
        def _():
            for k in range(2):
                alln_ref[later * 2 + k] = jnp.zeros(kvn_ref.shape, BF16)

    for d in range(1, n):
        r = (me + d) % n
        remote(meta_ref, allm_ref.at[r], meta_s.at[d], meta_r.at[r], r).wait_recv()

    def sends(l):
        return c % (2 ** (l + 1)) == 2**l - 1

    def targets(l):
        return [0] if l == 0 else list(range(1, 2**l, 2))

    def pre_copy(l, j, r):
        return remote(
            incl_ref.at[l, j],
            recv_ref.at[l, j],
            pre_s.at[l, j, r],
            pre_r.at[l, j],
            ((c + 1 + r) % n2) * 2 + i,
        )

    def relay_copy(l, j):
        return remote(
            recv_ref.at[l, j],
            recv_ref.at[l, j],
            rel_s.at[l, j],
            pre_r.at[l, j],
            ((c + n2 - 1) % n2) * 2 + i,
        )

    def logs(r, j):
        return allm_ref[r, :, lanes(i * half + j * size, size)]

    def gather_first(j, _):
        sib_copy(j).wait_recv()
        mine = state_ref[:, lanes(i * half + j * size, size)].astype(F32)
        theirs = sib_ref[j].astype(F32)
        d1 = jnp.exp2(logs(2 * c + 1, j))
        total = jnp.where(i == 0, d1 * mine + theirs, d1 * theirs + mine)
        incl_ref[0, j] = total.astype(BF16)
        own_ref[j] = jnp.zeros(own_ref.shape[1:], F32)

        @pl.when(sends(0))
        def _():
            pre_copy(0, j, 0).start()

        return 0

    lax.fori_loop(0, chunks, gather_first, 0)

    def forward(kind, d):
        src = allc_ref if kind == 0 else alln_ref
        slot = ((c + d) % n2) * 2 + i
        return remote(
            src.at[slot], src.at[slot], kv_f.at[kind, d], kv_r.at[kind, slot], other
        )

    def combine(j, _):
        for l in range(levels):

            @pl.when(c % (2 ** (l + 1)) >= 2**l)
            def _():
                pre_copy(l, j, 0).wait_recv()
                if l >= 1:

                    @pl.when(c % 2 == 1)
                    def _():
                        relay_copy(l, j).start()

                base = c - c % (2**l)
                logsum = jnp.zeros((1, size), F32)
                for back in range(1, 2**l):
                    at = (c + n2 - back) % n2
                    both = logs(2 * at, j) + logs(2 * at + 1, j)
                    logsum += jnp.where(c - back >= base, both, 0.0)
                own_ref[j] = jnp.exp2(logsum) * recv_ref[l, j].astype(F32) + own_ref[j]

            if l + 1 < levels:

                @pl.when(sends(l + 1))
                def _():
                    keep = jnp.exp2(logs(2 * c, j) + logs(2 * c + 1, j))
                    incl_ref[l + 1, j] = (
                        keep * own_ref[j] + incl_ref[0, j].astype(F32)
                    ).astype(BF16)
                    for r in targets(l + 1):
                        pre_copy(l + 1, j, r).start()

        enter = own_ref[j]
        mine = state_ref[:, lanes(i * half + j * size, size)].astype(F32)
        first = jnp.where(i == 0, mine, sib_ref[j].astype(F32))
        middle = jnp.exp2(logs(2 * c, j)) * enter + first
        out_ref[:, lanes(i * half + j * size, size)] = jnp.where(
            i == 0, enter, middle
        ).astype(BF16)
        back_ref[j] = jnp.where(i == 0, middle, enter).astype(BF16)
        back_copy(j, i).start()
        for d in range(1, n2):

            @pl.when(j == ((d * chunks) // n2))
            def _():
                remote_slot(0, d).wait_recv()
                forward(0, d).start()

                @pl.when((c + d) % n2 < c)
                def _():
                    remote_slot(1, d).wait_recv()
                    forward(1, d).start()

        return 0

    def remote_slot(kind, d):
        src = allc_ref if kind == 0 else alln_ref
        mine = kvc_ref if kind == 0 else kvn_ref
        slot = ((c + d) % n2) * 2 + i
        return remote(mine, src.at[slot], kv_s.at[kind, d], kv_r.at[kind, slot], slot)

    def back_copy(j, who):
        return remote(
            back_ref.at[j],
            out_ref.at[:, lanes(who * half + j * size, size)],
            back_s.at[j],
            back_r.at[j],
            other,
        )

    lax.fori_loop(0, chunks, combine, 0)

    def other_slot(kind, d):
        src = allc_ref if kind == 0 else alln_ref
        mine = kvc_ref if kind == 0 else kvn_ref
        slot = ((c + d) % n2) * 2 + (1 - i)
        return remote(mine, src.at[slot], kv_f.at[kind, d], kv_r.at[kind, slot], other)

    for d in range(n2):
        other_slot(0, d).wait_recv()
    other_slot(1, 0).wait_recv()
    for d in range(1, n2):

        @pl.when((c + d) % n2 < c)
        def _():
            other_slot(1, d).wait_recv()

    def drain(j, _):
        back_copy(j, 1 - i).wait_recv()
        back_copy(j, i).wait_send()
        sib_copy(j).wait_send()
        for l in range(levels):

            @pl.when(sends(l))
            def _():
                for r in targets(l):
                    pre_copy(l, j, r).wait_send()

            if l >= 1:

                @pl.when((c % (2 ** (l + 1)) >= 2**l) & (c % 2 == 1))
                def _():
                    relay_copy(l, j).wait_send()

        return 0

    lax.fori_loop(0, chunks, drain, 0)
    for d in range(1, n):
        remote(
            meta_ref, allm_ref.at[me], meta_s.at[d], meta_r.at[me], (me + d) % n
        ).wait_send()
    cache_copy(0, other).wait_send()
    new_copy(0, other).wait_send()
    for d in range(1, n2):
        to = ((c + d) % n2) * 2 + i
        cache_copy(d, to).wait_send()
        forward(0, d).wait_send()

        @pl.when(c + d < n2)
        def _():
            new_copy(d, to).wait_send()

        @pl.when((c + d) % n2 < c)
        def _():
            forward(1, d).wait_send()


def final_kernel(
    part_ref,
    fade_ref,
    sout_ref,
    state_ref,
    q_ref,
    kvc_ref,
    kvn_ref,
    meta_ref,
    nk_ref,
    y_ref,
    att_ref,
    code_ref,
    scale_ref,
    vc_ref,
    vn_ref,
    bias_ref,
):
    tokens, width = part_ref.shape
    heads = width // HEAD_DIM
    per_group = min(SSM_HEADS // GROUPS, heads)
    me, z = lax.axis_index("seq"), lax.axis_index("head")
    group0 = z * heads // (SSM_HEADS // GROUPS)
    block = min(512, width)

    magnitude = jnp.max(meta_ref[:, 0, width:], axis=0, keepdims=True)
    scale = (magnitude + 1e-6) / 127.0
    scale_ref[...] = scale
    code_ref[...] = (nk_ref[...].astype(F32) / scale).astype(BF16)

    def columns(b, _):
        here = lanes(b * block, block)
        g = group0 + (b * block) // (per_group * HEAD_DIM)
        prior = jnp.dot(
            sout_ref[:, lanes(g * STATE, STATE)], state_ref[:, here], preferred_element_type=F32
        )
        y = part_ref[:, here].astype(F32) + fade_ref[:, here].astype(F32) * prior
        y_ref[:, here] = y.astype(BF16)
        return 0

    lax.fori_loop(0, width // block, columns, 0)

    q_heads = q_ref.shape[1] // ATT_DIM
    kvw = kvc_ref.shape[1] // 2
    kv_here = kvw // ATT_DIM
    share = q_heads // kv_here
    fresh = kvn_ref.shape[0]
    for k in range(kv_here):
        at = kvw + k * ATT_DIM
        vc_ref[k, :, :ATT_DIM] = kvc_ref[:, at : at + ATT_DIM]
        vc_ref[k, :, ATT_DIM:] = jnp.ones((kvc_ref.shape[0], ATT_DIM), BF16)
        vn_ref[k, :, :ATT_DIM] = kvn_ref[:, at : at + ATT_DIM]
        vn_ref[k, :, ATT_DIM:] = jnp.ones((fresh, ATT_DIM), BF16)
    seen = iota((tokens, fresh), 1) <= me * tokens + iota((tokens, fresh), 0)
    bias_ref[...] = jnp.where(seen, 0.0, NEG)
    factor = ATT_DIM**-0.5 * LOG2E
    nt = (((1,), (1,)), ((), ()))

    def attend(h, _):
        k = h // share
        q = q_ref[:, lanes(h * ATT_DIM, ATT_DIM)]
        at = lanes(k * ATT_DIM, ATT_DIM)
        old = lax.dot_general(q, kvc_ref[:, at], nt, preferred_element_type=F32)
        new = lax.dot_general(q, kvn_ref[:, at], nt, preferred_element_type=F32) + bias_ref[...]
        peak = jnp.maximum(
            jnp.max(old, axis=1, keepdims=True), jnp.max(new, axis=1, keepdims=True)
        )
        old = jnp.exp2((old - peak) * factor).astype(BF16)
        new = jnp.exp2((new - peak) * factor).astype(BF16)
        both = jnp.dot(old, vc_ref[k], preferred_element_type=F32) + jnp.dot(
            new, vn_ref[k], preferred_element_type=F32
        )
        att_ref[:, lanes(h * ATT_DIM, ATT_DIM)] = (
            both[:, :ATT_DIM] / both[:, ATT_DIM:]
        ).astype(BF16)
        return 0

    lax.fori_loop(0, q_heads, attend, 0)


def body(
    n,
    ssm_input,
    state_in,
    state_out,
    step_size,
    decay_rate,
    forget,
    skip_gain,
    queries,
    new_keys,
    new_values,
    cache_keys,
    cache_values,
    cache_key_scale,
    cache_value_scale,
):
    tokens, width = ssm_input.shape
    heads = step_size.shape[1]
    rows = cache_keys.shape[0]
    channels = new_keys.shape[1]
    q_heads = queries.shape[1] // ATT_DIM
    kv_here = max(1, q_heads // (ATT_HEADS // KV_HEADS))
    kvw = kv_here * ATT_DIM
    per_group = min(SSM_HEADS // GROUPS, heads)
    groups_here = heads // per_group
    limit = pltpu.CompilerParams(vmem_limit_bytes=60 * 1024 * 1024)
    shape = jax.ShapeDtypeStruct
    state, part, fade, meta, kvc, kvn = pl.pallas_call(
        local_kernel,
        out_shape=(
            shape((STATE, width), BF16),
            shape((tokens, width), BF16),
            shape((tokens, width), BF16),
            shape((1, width + channels), F32),
            shape((rows, 2 * kvw), BF16),
            shape((tokens, 2 * kvw), BF16),
        ),
        in_specs=[VMEM] * 13,
        out_specs=(VMEM,) * 6,
        scratch_shapes=[
            pltpu.VMEM((groups_here, tokens, tokens), F32),
            pltpu.VMEM((groups_here, STATE, tokens), BF16),
            pltpu.VMEM((heads, tokens), F32),
        ],
        compiler_params=limit,
        name="local",
    )(
        ssm_input,
        state_in,
        state_out,
        step_size,
        decay_rate.reshape(1, heads),
        forget.reshape(tokens, 1),
        jnp.repeat(skip_gain, HEAD_DIM).reshape(1, width),
        new_keys,
        new_values,
        cache_keys,
        cache_values,
        cache_key_scale.reshape(1, channels),
        cache_value_scale.reshape(1, channels),
    )
    half = width // 2
    size = min(256, half)
    chunks = half // size
    n2 = n // 2
    levels = n2.bit_length() - 1
    fan = max(1, n2 // 2)
    dma = pltpu.SemaphoreType.DMA
    carried, allc, alln, allm = pl.pallas_call(
        functools.partial(comm_kernel, n, chunks),
        out_shape=(
            shape((STATE, width), BF16),
            shape((n, rows, 2 * kvw), BF16),
            shape((n, tokens, 2 * kvw), BF16),
            shape((n, 1, width + channels), F32),
        ),
        in_specs=[VMEM] * 4,
        out_specs=(VMEM,) * 4,
        scratch_shapes=[
            pltpu.VMEM((chunks, STATE, size), BF16),
            pltpu.VMEM((chunks, STATE, size), F32),
            pltpu.VMEM((levels, chunks, STATE, size), BF16),
            pltpu.VMEM((levels, chunks, STATE, size), BF16),
            pltpu.VMEM((chunks, STATE, size), BF16),
            dma((n,)),
            dma((n,)),
            dma((2, n2)),
            dma((2, n)),
            dma((2, n2)),
            dma((chunks,)),
            dma((chunks,)),
            dma((levels, chunks, fan)),
            dma((levels, chunks)),
            dma((levels, chunks)),
            dma((chunks,)),
            dma((chunks,)),
        ],
        compiler_params=pltpu.CompilerParams(
            collective_id=0, has_side_effects=True, vmem_limit_bytes=60 * 1024 * 1024
        ),
        name="exchange",
    )(state, kvc, kvn, meta)
    y, attended, codes, scale = pl.pallas_call(
        final_kernel,
        out_shape=(
            shape((tokens, width), BF16),
            shape((tokens, queries.shape[1]), BF16),
            shape((tokens, channels), BF16),
            shape((1, channels), F32),
        ),
        in_specs=[VMEM] * 9,
        out_specs=(VMEM,) * 4,
        scratch_shapes=[
            pltpu.VMEM((kv_here, n * rows, 2 * ATT_DIM), BF16),
            pltpu.VMEM((kv_here, n * tokens, 2 * ATT_DIM), BF16),
            pltpu.VMEM((tokens, n * tokens), F32),
        ],
        compiler_params=limit,
        name="finish",
    )(
        part,
        fade,
        state_out,
        carried,
        queries,
        allc.reshape(n * rows, 2 * kvw),
        alln.reshape(n * tokens, 2 * kvw),
        allm,
        new_keys,
    )
    return (y, attended, codes, scale.reshape(channels))


def solution(mesh):
    in_specs = (
        P("seq", "head"),
        P("seq", None),
        P("seq", None),
        P("seq", "head"),
        P("head"),
        P("seq"),
        P("head"),
        P("seq", "head"),
        P("seq", None),
        P("seq", None),
        P("seq", None),
        P("seq", None),
        P(),
        P(),
    )
    out_specs = (P("seq", "head"), P("seq", "head"), P("seq", None), P())
    return jax.shard_map(
        functools.partial(body, mesh.shape["seq"]),
        mesh=mesh,
        in_specs=in_specs,
        out_specs=out_specs,
        check_vma=False,
    )
```

profile of v0, /device:TPU:29, one launch (start us, length us, event | category | flops | bytes accessed | tf_op | source)
XLA Modules:
  0.0 116.2 jit_solution(6640102365167795460)
XLA Ops:
  0.6 0.7 broadcast_in_dim.3
  1.4 0.7 reshape_reshape.3.skip_ref
  2.0 1.6 %copy.19.step_ref = f32[192,64]{1,0:T(8,128)} copy(f32[192,64]{0,1:T(8,128)} %param.17) | data formatting | bytes 98304 | tf_op args[3]
  3.6 1.4 %copy.20.forget_ref = f32[192,1]{1,0:T(8,128)} copy(f32[192,1]{0,1:T(1,128)} %bitcast.11) | data formatting | bytes 1536 | tf_op jit(solution)/shard_map/reshape | solution.py:538
  5.1 24.1 %local.1 = (bf16[256,4096]{1,0:T(8,128)(2,1)}, bf16[192,4096]{1,0:T(8,128)(2,1)}, bf16[192,4096]{1,0:T(8,128)(2,1)}, f32[1,5120]{1,0:T(1,128)}, bf16[128,512]{1,0:T(8,128)(2,1)}, /*index=5*/bf16[192,512]{1,0:T(8,128)(2,1)}) custom-call(bf16[192,4096]{1,0:T(8,128)(2,1)} %x_ref.1, bf16[192,2048]{1,0:T(8,128)(2,1)} %sin_ref.1, bf16[192,2048]{1,0:T(8,128)(2,1)} %sout_ref.3, ...), custom_call_target="tpu_custom_call" | custom-call | tf_op jit(solution)/shard_map/local/pallas_call | solution.py:513
  29.2 57.9 %exchange.1 = (bf16[256,4096]{1,0:T(8,128)(2,1)}, bf16[8,128,512]{2,1,0:T(8,128)(2,1)}, bf16[8,192,512]{2,1,0:T(8,128)(2,1)}, f32[8,1,5120]{2,1,0:T(1,128)}) custom-call(bf16[256,4096]{1,0:T(8,128)(2,1)} %get-tuple-element.20.state_ref, bf16[128,512]{1,0:T(8,128)(2,1)} %get-tuple-element.21.kvc_ref, bf16[192,512]{1,0:T(8,128)(2,1)} %get-tuple-element.22.kvn_ref, ...), custom_call_target="tpu_custom_call" | custom-call | tf_op jit(solution)/shard_map/exchange/pallas_call | solution.py:554
  87.1 29.1 %finish.1 = (bf16[192,4096]{1,0:T(8,128)(2,1)}, bf16[192,2048]{1,0:T(8,128)(2,1)}, bf16[192,1024]{1,0:T(8,128)(2,1)}, f32[1,1024]{1,0:T(1,128)}) custom-call(bf16[192,4096]{1,0:T(8,128)(2,1)} %get-tuple-element.18.part_ref, bf16[192,4096]{1,0:T(8,128)(2,1)} %get-tuple-element.19.fade_ref, bf16[192,2048]{1,0:T(8,128)(2,1)} %sout_ref.3, ...), custom_call_target="tpu_custom_call" | custom-call | tf_op jit(solution)/shard_map/finish/pallas_call | solution.py:588
where the time goes:
time: 116 us
  Pallas kernels  111 us (96%)
  local copies, waits for them, and re-layouts  4.44 us (4%)
    pallas_call x1, Pallas kernels, body(): pl.pallas_call(functools.partial(comm_kernel, n, chunks), out_shape=(shap...  57.9 us
    pallas_call x1, Pallas kernels, body(): pl.pallas_call(final_kernel, out_shape=(shape((tokens, width), BF16), sha...  29.1 us
    pallas_call x1, Pallas kernels, body(): pl.pallas_call(local_kernel, out_shape=(shape((STATE, width), BF16), shap...  24.1 us

commit v1 on v0

--- a/solution.py
+++ b/solution.py
@@ -46,17 +46,15 @@
     cks_ref,
     cvs_ref,
     state_ref,
-    part_ref,
-    fade_ref,
+    run_ref,
+    at_ref,
+    gram_ref,
     meta_ref,
     kvc_ref,
     kvn_ref,
-    gram_ref,
-    bt_ref,
-    at_ref,
 ):
     tokens, width = x_ref.shape
-    heads = step_ref.shape[1]
+    heads = step_ref.shape[0]
     per_group = min(SSM_HEADS // GROUPS, heads)
     groups_here = heads // per_group
     z = lax.axis_index("head")
@@ -71,56 +69,97 @@
     kvn_ref[:, kvw:] = nv_ref[:, cols]
     meta_ref[:, width:] = jnp.max(jnp.abs(nk_ref[...].astype(F32)), axis=0, keepdims=True)
 
-    rate = (-decay_ref[...] * step_ref[...] - forget_ref[...]) * LOG2E
     row, col = iota((tokens, tokens), 0), iota((tokens, tokens), 1)
     lower = jnp.where(col <= row, 1.0, 0.0)
     eye = jnp.where(col == row, 1.0, 0.0)
-    running = jnp.dot(lower, rate, precision=HIGHEST, preferred_element_type=F32)
-    lstep = jnp.log2(step_ref[...])
-    start = running - lstep
-    at_ref[...] = lax.dot_general(
-        start, eye, (((0,), (0,)), ((), ())), precision=HIGHEST, preferred_element_type=F32
+    step = step_ref[...].T
+    forgotten = jnp.sum(lower * forget_ref[...], axis=1, keepdims=True)
+    decayed = jnp.dot(
+        lower, decay_ref[...] * step, precision=HIGHEST, preferred_element_type=F32
     )
+    running = -(decayed + forgotten) * LOG2E
+    start = running - jnp.log2(step)
+    at_ref[...] = start.T
+    run_ref[:tokens] = running
+    run_ref[tokens:] = jnp.broadcast_to(skip_ref[...], (8, heads))
     tail = jnp.exp2(running[tokens - 1 : tokens] - start).astype(BF16)
+    last = running[tokens - 8 : tokens]
+    block = min(512, width)
     for g in range(groups_here):
         gcols = lanes((group0 + g) * STATE, STATE)
         maps_in = sin_ref[:, gcols]
         gram_ref[g] = lax.dot_general(
             sout_ref[:, gcols], maps_in, (((1,), (1,)), ((), ())), preferred_element_type=F32
         )
-        bt_ref[g] = lax.dot_general(
+        turned = lax.dot_general(
             maps_in,
             eye.astype(BF16),
             (((0,), (0,)), ((), ())),
             preferred_element_type=F32,
         ).astype(BF16)
-
-    def pair(p, _):
-        here = lanes(p * 128, 128)
-        g = (2 * p) // per_group
-        pick = (iota((heads, 128), 0) == 2 * p + iota((heads, 128), 1) // HEAD_DIM).astype(F32)
-        run = jnp.dot(running, pick, precision=HIGHEST, preferred_element_type=F32)
-        meta_ref[:, here] = run[tokens - 1 : tokens]
-        fade_ref[:, here] = jnp.exp2(run).astype(BF16)
-        x = x_ref[:, here]
-        scale = jnp.dot(tail, pick.astype(BF16), preferred_element_type=F32)
-        scaled = (x.astype(F32) * scale).astype(BF16)
-        state_ref[:, here] = jnp.dot(
-            bt_ref[g], scaled, preferred_element_type=F32
-        ).astype(BF16)
-        gram = gram_ref[g]
-        causal = iota((tokens, tokens), 1) <= iota((tokens, tokens), 0)
-
-        def one(k):
-            spread = run[:, k * HEAD_DIM : k * HEAD_DIM + 1] - at_ref[pl.ds(2 * p + k, 1), :]
-            weight = jnp.exp2(jnp.where(causal, spread, NEG)) * gram
-            return jnp.dot(weight.astype(BF16), x, preferred_element_type=F32)
-
-        y = jnp.where(iota((tokens, 128), 1) < HEAD_DIM, one(0), one(1))
-        part_ref[:, here] = (y + skip_ref[:, here] * x.astype(F32)).astype(BF16)
-        return 0
-
-    lax.fori_loop(0, heads // 2, pair, 0)
+        for b in range(per_group * HEAD_DIM // block):
+            begin = g * per_group * HEAD_DIM + b * block
+            here = pl.ds(begin, block)
+            pick = choose(heads, begin, block)
+            meta_ref[:, here] = jnp.dot(
+                last, pick, precision=HIGHEST, preferred_element_type=F32
+            )[7:8]
+            scale = jnp.dot(tail, pick.astype(BF16), preferred_element_type=F32)
+            scaled = (x_ref[:, here].astype(F32) * scale).astype(BF16)
+            state_ref[:, here] = jnp.dot(
+                turned, scaled, preferred_element_type=F32
+            ).astype(BF16)
+
+
+def choose(heads, begin, size):
+    lane = begin + iota((heads, size), 1)
+    return (iota((heads, size), 0) == lane // HEAD_DIM).astype(F32)
+
+
+def within_pair(p, x_ref, run_ref, at_ref, gram_ref, part_ref):
+    tokens = x_ref.shape[0]
+    heads = run_ref.shape[1]
+    per_group = min(SSM_HEADS // GROUPS, heads)
+    here = lanes(p * 128, 128)
+    pick = choose(heads, p * 128, 128)
+    both = jnp.dot(run_ref[...], pick, precision=HIGHEST, preferred_element_type=F32)
+    run, skip = both[:tokens], both[tokens : tokens + 1]
+    x = x_ref[:, here]
+    gram = gram_ref[(2 * p) // per_group]
+    causal = iota((tokens, tokens), 1) <= iota((tokens, tokens), 0)
+
+    def one(k):
+        spread = run[:, k * HEAD_DIM : k * HEAD_DIM + 1] - at_ref[pl.ds(2 * p + k, 1), :]
+        weight = jnp.exp2(jnp.where(causal, spread, NEG)) * gram
+        return jnp.dot(weight.astype(BF16), x, preferred_element_type=F32)
+
+    y = jnp.where(iota((tokens, 128), 1) < HEAD_DIM, one(0), one(1))
+    part_ref[:, here] = (y + skip * x.astype(F32)).astype(BF16)
+
+
+def attend(h, q_ref, allc_ref, alln_ref, bias_ref, vc_ref, vn_ref, att_ref):
+    q_heads = q_ref.shape[1] // ATT_DIM
+    kv_here = vc_ref.shape[0]
+    k = h // (q_heads // kv_here)
+    factor = ATT_DIM**-0.5 * LOG2E
+    nt = (((1,), (1,)), ((), ()))
+    q = q_ref[:, lanes(h * ATT_DIM, ATT_DIM)]
+    at = lanes(k * ATT_DIM, ATT_DIM)
+    keys_c = allc_ref[:, :, at].reshape(-1, ATT_DIM)
+    keys_n = alln_ref[:, :, at].reshape(-1, ATT_DIM)
+    old = lax.dot_general(q, keys_c, nt, preferred_element_type=F32)
+    new = lax.dot_general(q, keys_n, nt, preferred_element_type=F32) + bias_ref[...]
+    peak = jnp.maximum(
+        jnp.max(old, axis=1, keepdims=True), jnp.max(new, axis=1, keepdims=True)
+    )
+    old = jnp.exp2((old - peak) * factor).astype(BF16)
+    new = jnp.exp2((new - peak) * factor).astype(BF16)
+    both = jnp.dot(old, vc_ref[k], preferred_element_type=F32) + jnp.dot(
+        new, vn_ref[k], preferred_element_type=F32
+    )
+    att_ref[:, lanes(h * ATT_DIM, ATT_DIM)] = (
+        both[:, :ATT_DIM] / both[:, ATT_DIM:]
+    ).astype(BF16)
 
 
 def comm_kernel(
@@ -130,10 +169,20 @@
     kvc_ref,
     kvn_ref,
     meta_ref,
+    x_ref,
+    run_ref,
+    at_ref,
+    gram_ref,
+    q_ref,
     out_ref,
+    allm_ref,
+    part_ref,
+    att_ref,
     allc_ref,
     alln_ref,
-    allm_ref,
+    vc_ref,
+    vn_ref,
+    bias_ref,
     sib_ref,
     own_ref,
     incl_ref,
@@ -268,6 +317,12 @@
         return 0
 
     lax.fori_loop(0, chunks, gather_first, 0)
+    fresh = bias_ref.shape[1]
+    tokens = x_ref.shape[0]
+    seen = iota((tokens, fresh), 1) <= me * tokens + iota((tokens, fresh), 0)
+    bias_ref[...] = jnp.where(seen, 0.0, NEG)
+    early = max(1, chunks // 2)
+    late = max(1, chunks - early)
 
     def forward(kind, d):
         src = allc_ref if kind == 0 else alln_ref
@@ -316,18 +371,6 @@
         ).astype(BF16)
         back_ref[j] = jnp.where(i == 0, middle, enter).astype(BF16)
         back_copy(j, i).start()
-        for d in range(1, n2):
-
-            @pl.when(j == ((d * chunks) // n2))
-            def _():
-                remote_slot(0, d).wait_recv()
-                forward(0, d).start()
-
-                @pl.when((c + d) % n2 < c)
-                def _():
-                    remote_slot(1, d).wait_recv()
-                    forward(1, d).start()
-
         return 0
 
     def remote_slot(kind, d):
@@ -345,7 +388,30 @@
             other,
         )
 
-    lax.fori_loop(0, chunks, combine, 0)
+    def first_part(j, _):
+        pairs = width // 128
+
+        def pair(p, _):
+            within_pair(p, x_ref, run_ref, at_ref, gram_ref, part_ref)
+            return 0
+
+        lax.fori_loop(j * pairs // early, (j + 1) * pairs // early, pair, 0)
+        combine(j, 0)
+        for d in range(1, n2):
+
+            @pl.when(j == (d * early) // n2)
+            def _():
+                remote_slot(0, d).wait_recv()
+                forward(0, d).start()
+
+                @pl.when((c + d) % n2 < c)
+                def _():
+                    remote_slot(1, d).wait_recv()
+                    forward(1, d).start()
+
+        return 0
+
+    lax.fori_loop(0, early, first_part, 0)
 
     def other_slot(kind, d):
         src = allc_ref if kind == 0 else alln_ref
@@ -361,6 +427,30 @@
         @pl.when((c + d) % n2 < c)
         def _():
             other_slot(1, d).wait_recv()
+
+    kv_here = vc_ref.shape[0]
+    for k in range(kv_here):
+        at = (kv_here + k) * ATT_DIM
+        for all_ref, ext_ref in ((allc_ref, vc_ref), (alln_ref, vn_ref)):
+            ext_ref[k, :, :ATT_DIM] = all_ref[:, :, at : at + ATT_DIM].reshape(-1, ATT_DIM)
+            ext_ref[k, :, ATT_DIM:] = jnp.ones((ext_ref.shape[1], ATT_DIM), BF16)
+
+    def second_part(j, _):
+        q_heads = q_ref.shape[1] // ATT_DIM
+
+        def head(h, _):
+            attend(h, q_ref, allc_ref, alln_ref, bias_ref, vc_ref, vn_ref, att_ref)
+            return 0
+
+        lax.fori_loop(j * q_heads // late, (j + 1) * q_heads // late, head, 0)
+
+        @pl.when(early + j < chunks)
+        def _():
+            combine(early + j, 0)
+
+        return 0
+
+    lax.fori_loop(0, late, second_part, 0)
 
     def drain(j, _):
         back_copy(j, 1 - i).wait_recv()
@@ -404,26 +494,19 @@
 
 def final_kernel(
     part_ref,
-    fade_ref,
+    run_ref,
     sout_ref,
     state_ref,
-    q_ref,
-    kvc_ref,
-    kvn_ref,
     meta_ref,
     nk_ref,
     y_ref,
-    att_ref,
     code_ref,
     scale_ref,
-    vc_ref,
-    vn_ref,
-    bias_ref,
 ):
     tokens, width = part_ref.shape
-    heads = width // HEAD_DIM
+    heads = run_ref.shape[1]
     per_group = min(SSM_HEADS // GROUPS, heads)
-    me, z = lax.axis_index("seq"), lax.axis_index("head")
+    z = lax.axis_index("head")
     group0 = z * heads // (SSM_HEADS // GROUPS)
     block = min(512, width)
 
@@ -431,55 +514,16 @@
     scale = (magnitude + 1e-6) / 127.0
     scale_ref[...] = scale
     code_ref[...] = (nk_ref[...].astype(F32) / scale).astype(BF16)
-
-    def columns(b, _):
-        here = lanes(b * block, block)
+    fade = jnp.exp2(run_ref[:tokens]).astype(BF16)
+    for b in range(width // block):
+        here = pl.ds(b * block, block)
         g = group0 + (b * block) // (per_group * HEAD_DIM)
         prior = jnp.dot(
             sout_ref[:, lanes(g * STATE, STATE)], state_ref[:, here], preferred_element_type=F32
         )
-        y = part_ref[:, here].astype(F32) + fade_ref[:, here].astype(F32) * prior
-        y_ref[:, here] = y.astype(BF16)
-        return 0
-
-    lax.fori_loop(0, width // block, columns, 0)
-
-    q_heads = q_ref.shape[1] // ATT_DIM
-    kvw = kvc_ref.shape[1] // 2
-    kv_here = kvw // ATT_DIM
-    share = q_heads // kv_here
-    fresh = kvn_ref.shape[0]
-    for k in range(kv_here):
-        at = kvw + k * ATT_DIM
-        vc_ref[k, :, :ATT_DIM] = kvc_ref[:, at : at + ATT_DIM]
-        vc_ref[k, :, ATT_DIM:] = jnp.ones((kvc_ref.shape[0], ATT_DIM), BF16)
-        vn_ref[k, :, :ATT_DIM] = kvn_ref[:, at : at + ATT_DIM]
-        vn_ref[k, :, ATT_DIM:] = jnp.ones((fresh, ATT_DIM), BF16)
-    seen = iota((tokens, fresh), 1) <= me * tokens + iota((tokens, fresh), 0)
-    bias_ref[...] = jnp.where(seen, 0.0, NEG)
-    factor = ATT_DIM**-0.5 * LOG2E
-    nt = (((1,), (1,)), ((), ()))
-
-    def attend(h, _):
-        k = h // share
-        q = q_ref[:, lanes(h * ATT_DIM, ATT_DIM)]
-        at = lanes(k * ATT_DIM, ATT_DIM)
-        old = lax.dot_general(q, kvc_ref[:, at], nt, preferred_element_type=F32)
-        new = lax.dot_general(q, kvn_ref[:, at], nt, preferred_element_type=F32) + bias_ref[...]
-        peak = jnp.maximum(
-            jnp.max(old, axis=1, keepdims=True), jnp.max(new, axis=1, keepdims=True)
-        )
-        old = jnp.exp2((old - peak) * factor).astype(BF16)
-        new = jnp.exp2((new - peak) * factor).astype(BF16)
-        both = jnp.dot(old, vc_ref[k], preferred_element_type=F32) + jnp.dot(
-            new, vn_ref[k], preferred_element_type=F32
-        )
-        att_ref[:, lanes(h * ATT_DIM, ATT_DIM)] = (
-            both[:, :ATT_DIM] / both[:, ATT_DIM:]
-        ).astype(BF16)
-        return 0
-
-    lax.fori_loop(0, q_heads, attend, 0)
+        pick = choose(heads, b * block, block).astype(BF16)
+        spread = jnp.dot(fade, pick, preferred_element_type=F32)
+        y_ref[:, here] = (part_ref[:, here].astype(F32) + spread * prior).astype(BF16)
 
 
 def body(
@@ -510,33 +554,29 @@
     groups_here = heads // per_group
     limit = pltpu.CompilerParams(vmem_limit_bytes=60 * 1024 * 1024)
     shape = jax.ShapeDtypeStruct
-    state, part, fade, meta, kvc, kvn = pl.pallas_call(
+    state, run, at, gram, meta, kvc, kvn = pl.pallas_call(
         local_kernel,
         out_shape=(
             shape((STATE, width), BF16),
-            shape((tokens, width), BF16),
-            shape((tokens, width), BF16),
+            shape((tokens + 8, heads), F32),
+            shape((heads, tokens), F32),
+            shape((groups_here, tokens, tokens), F32),
             shape((1, width + channels), F32),
             shape((rows, 2 * kvw), BF16),
             shape((tokens, 2 * kvw), BF16),
         ),
         in_specs=[VMEM] * 13,
-        out_specs=(VMEM,) * 6,
-        scratch_shapes=[
-            pltpu.VMEM((groups_here, tokens, tokens), F32),
-            pltpu.VMEM((groups_here, STATE, tokens), BF16),
-            pltpu.VMEM((heads, tokens), F32),
-        ],
+        out_specs=(VMEM,) * 7,
         compiler_params=limit,
         name="local",
     )(
         ssm_input,
         state_in,
         state_out,
-        step_size,
+        step_size.T,
         decay_rate.reshape(1, heads),
-        forget.reshape(tokens, 1),
-        jnp.repeat(skip_gain, HEAD_DIM).reshape(1, width),
+        forget.reshape(1, tokens),
+        skip_gain.reshape(1, heads),
         new_keys,
         new_values,
         cache_keys,
@@ -551,17 +591,22 @@
     levels = n2.bit_length() - 1
     fan = max(1, n2 // 2)
     dma = pltpu.SemaphoreType.DMA
-    carried, allc, alln, allm = pl.pallas_call(
+    carried, allm, part, attended = pl.pallas_call(
         functools.partial(comm_kernel, n, chunks),
         out_shape=(
             shape((STATE, width), BF16),
-            shape((n, rows, 2 * kvw), BF16),
-            shape((n, tokens, 2 * kvw), BF16),
             shape((n, 1, width + channels), F32),
+            shape((tokens, width), BF16),
+            shape((tokens, queries.shape[1]), BF16),
         ),
-        in_specs=[VMEM] * 4,
+        in_specs=[VMEM] * 9,
         out_specs=(VMEM,) * 4,
         scratch_shapes=[
+            pltpu.VMEM((n, rows, 2 * kvw), BF16),
+            pltpu.VMEM((n, tokens, 2 * kvw), BF16),
+            pltpu.VMEM((kv_here, n * rows, 2 * ATT_DIM), BF16),
+            pltpu.VMEM((kv_here, n * tokens, 2 * ATT_DIM), BF16),
+            pltpu.VMEM((tokens, n * tokens), F32),
             pltpu.VMEM((chunks, STATE, size), BF16),
             pltpu.VMEM((chunks, STATE, size), F32),
             pltpu.VMEM((levels, chunks, STATE, size), BF16),
@@ -584,35 +629,19 @@
             collective_id=0, has_side_effects=True, vmem_limit_bytes=60 * 1024 * 1024
         ),
         name="exchange",
-    )(state, kvc, kvn, meta)
-    y, attended, codes, scale = pl.pallas_call(
+    )(state, kvc, kvn, meta, ssm_input, run, at, gram, queries)
+    y, codes, scale = pl.pallas_call(
         final_kernel,
         out_shape=(
             shape((tokens, width), BF16),
-            shape((tokens, queries.shape[1]), BF16),
             shape((tokens, channels), BF16),
             shape((1, channels), F32),
         ),
-        in_specs=[VMEM] * 9,
-        out_specs=(VMEM,) * 4,
-        scratch_shapes=[
-            pltpu.VMEM((kv_here, n * rows, 2 * ATT_DIM), BF16),
-            pltpu.VMEM((kv_here, n * tokens, 2 * ATT_DIM), BF16),
-            pltpu.VMEM((tokens, n * tokens), F32),
-        ],
+        in_specs=[VMEM] * 6,
+        out_specs=(VMEM,) * 3,
         compiler_params=limit,
         name="finish",
-    )(
-        part,
-        fade,
-        state_out,
-        carried,
-        queries,
-        allc.reshape(n * rows, 2 * kvw),
-        alln.reshape(n * tokens, 2 * kvw),
-        allm,
-        new_keys,
-    )
+    )(part, run, state_out, carried, allm, new_keys)
     return (y, attended, codes, scale.reshape(channels))
 
 

time: 116 us -> 92.3 us (0.80)
  Pallas kernels: 111 us -> 90.6 us
  local copies, waits for them, and re-layouts: 4.44 us -> 0.88 us
    pallas_call x1, Pallas kernels: 29.1 us -> 4.8 us  [body(): pl.pallas_call(final_kernel, out_shape=(shape((tokens, width), BF16), sha...]
    pallas_call x1, Pallas kernels: 57.9 us -> 79.1 us  [body(): pl.pallas_call(functools.partial(comm_kernel, n, chunks), out_shape=(shap...]
    pallas_call x1, Pallas kernels: 24.1 us -> 6.72 us  [body(): pl.pallas_call(local_kernel, out_shape=(shape((STATE, width), BF16), shap...]
    reshape x1 -> x0, local copies, waits for them, and re-layouts: 1.45 us -> none  [body(): forget.reshape(tokens, 1)]
where the time goes in v1:
time: 92.3 us; the launch traced here: 92.2 us
  Pallas kernels  90.6 us (98%)
    pallas_call x1, Pallas kernels, body(): pl.pallas_call(functools.partial(comm_kernel, n, chunks), out_shape=(shap...  79.1 us
    pallas_call x1, Pallas kernels, body(): pl.pallas_call(local_kernel, out_shape=(shape((STATE, width), BF16), shap...  6.72 us
    pallas_call x1, Pallas kernels, body(): pl.pallas_call(final_kernel, out_shape=(shape((tokens, width), BF16), sha...  4.8 us

profile of v1, /device:TPU:29, one launch (start us, length us, event | category | flops | bytes accessed | tf_op | source)
XLA Modules:
  0.0 92.2 jit_solution(17396902123648158793)
XLA Ops:
  0.6 6.7 %local.1 = (bf16[256,4096]{1,0:T(8,128)(2,1)}, f32[200,64]{1,0:T(8,128)}, f32[64,192]{1,0:T(8,128)}, f32[2,192,192]{2,1,0:T(8,128)}, f32[1,5120]{1,0:T(1,128)}, ...) custom-call(bf16[192,4096]{1,0:T(8,128)(2,1)} %x_ref.3, bf16[192,2048]{1,0:T(8,128)(2,1)} %sin_ref.1, ...), custom_call_target="tpu_custom_call" | custom-call | tf_op jit(solution)/shard_map/local/pallas_call | solution.py:557
  7.4 79.1 %exchange.1 = (bf16[256,4096]{1,0:T(8,128)(2,1)}, f32[8,1,5120]{2,1,0:T(1,128)}, bf16[192,4096]{1,0:T(8,128)(2,1)}, bf16[192,2048]{1,0:T(8,128)(2,1)}) custom-call(bf16[256,4096]{1,0:T(8,128)(2,1)} %get-tuple-element.18.state_ref, bf16[128,512]{1,0:T(8,128)(2,1)} %get-tuple-element.19.kvc_ref, bf16[192,512]{1,0:T(8,128)(2,1)} %get-tuple-element.20.kvn_ref, ...), custom_call_target="tpu_custom_call" | custom-call | tf_op jit(solution)/shard_map/exchange/pallas_call | solution.py:594
  86.5 0.0 copy-start
  86.5 4.8 %finish.1 = (bf16[192,4096]{1,0:T(8,128)(2,1)}, bf16[192,1024]{1,0:T(8,128)(2,1)}, f32[1,1024]{1,0:T(1,128)}) custom-call(bf16[192,4096]{1,0:T(8,128)(2,1)} %get-tuple-element.25.part_ref, f32[200,64]{1,0:T(8,128)} %get-tuple-element.22.run_ref, bf16[192,2048]{1,0:T(8,128)(2,1)} %sout_ref.3, bf16[256,4096]{1,0:T(8,128)(2,1)} %get-tuple-element.26.state_ref, ...), custom_call_target="tpu_custom_call" | custom-call | tf_op jit(solution)/shard_map/finish/pallas_call | solution.py:633
  91.3 0.0 copy-done
  91.3 0.9 copy.19
Async XLA Ops:
  86.5 4.8 %copy-start = (bf16[192,2048]{1,0:T(8,128)(2,1)S(1)}, bf16[192,2048]{1,0:T(8,128)(2,1)}, u32[]{:S(2)}) copy-start(bf16[192,2048]{1,0:T(8,128)(2,1)} %get-tuple-element.37) | copy-start | bytes 2359300

commit v2 on v1

--- a/solution.py
+++ b/solution.py
@@ -47,6 +47,7 @@
     cvs_ref,
     state_ref,
     run_ref,
+    fade_ref,
     at_ref,
     gram_ref,
     meta_ref,
@@ -80,8 +81,14 @@
     running = -(decayed + forgotten) * LOG2E
     start = running - jnp.log2(step)
     at_ref[...] = start.T
-    run_ref[:tokens] = running
-    run_ref[tokens:] = jnp.broadcast_to(skip_ref[...], (8, heads))
+    rest = jnp.concatenate(
+        [running, jnp.broadcast_to(skip_ref[...], (16, heads))], axis=0
+    )
+    for third in range(3):
+        piece = rest.astype(BF16)
+        run_ref[:, third * heads : (third + 1) * heads] = piece
+        rest = rest - piece.astype(F32)
+    fade_ref[...] = jnp.exp2(running).astype(BF16)
     tail = jnp.exp2(running[tokens - 1 : tokens] - start).astype(BF16)
     last = running[tokens - 8 : tokens]
     block = min(512, width)
@@ -118,11 +125,13 @@
 
 def within_pair(p, x_ref, run_ref, at_ref, gram_ref, part_ref):
     tokens = x_ref.shape[0]
-    heads = run_ref.shape[1]
+    heads = run_ref.shape[1] // 3
     per_group = min(SSM_HEADS // GROUPS, heads)
     here = lanes(p * 128, 128)
-    pick = choose(heads, p * 128, 128)
-    both = jnp.dot(run_ref[...], pick, precision=HIGHEST, preferred_element_type=F32)
+    pick = choose(heads, p * 128, 128).astype(BF16)
+    both = jnp.dot(
+        run_ref[...], jnp.concatenate([pick] * 3, axis=0), preferred_element_type=F32
+    )
     run, skip = both[:tokens], both[tokens : tokens + 1]
     x = x_ref[:, here]
     gram = gram_ref[(2 * p) // per_group]
@@ -130,25 +139,33 @@
 
     def one(k):
         spread = run[:, k * HEAD_DIM : k * HEAD_DIM + 1] - at_ref[pl.ds(2 * p + k, 1), :]
-        weight = jnp.exp2(jnp.where(causal, spread, NEG)) * gram
-        return jnp.dot(weight.astype(BF16), x, preferred_element_type=F32)
-
-    y = jnp.where(iota((tokens, 128), 1) < HEAD_DIM, one(0), one(1))
+        return (jnp.exp2(jnp.where(causal, spread, NEG)) * gram).astype(BF16)
+
+    pair = jnp.dot(
+        jnp.concatenate([one(0), one(1)], axis=0), x, preferred_element_type=F32
+    )
+    y = jnp.where(iota((tokens, 128), 1) < HEAD_DIM, pair[:tokens], pair[tokens:])
     part_ref[:, here] = (y + skip * x.astype(F32)).astype(BF16)
 
 
 def attend(h, q_ref, allc_ref, alln_ref, bias_ref, vc_ref, vn_ref, att_ref):
     q_heads = q_ref.shape[1] // ATT_DIM
     kv_here = vc_ref.shape[0]
-    k = h // (q_heads // kv_here)
+    share = q_heads // kv_here
+    together = 2 if share % 2 == 0 else 1
+    tokens = q_ref.shape[0]
+    k = (h * together) // share
     factor = ATT_DIM**-0.5 * LOG2E
     nt = (((1,), (1,)), ((), ()))
-    q = q_ref[:, lanes(h * ATT_DIM, ATT_DIM)]
+    own = [lanes((h * together + e) * ATT_DIM, ATT_DIM) for e in range(together)]
+    q = jnp.concatenate([q_ref[:, o] for o in own], axis=0)
     at = lanes(k * ATT_DIM, ATT_DIM)
     keys_c = allc_ref[:, :, at].reshape(-1, ATT_DIM)
     keys_n = alln_ref[:, :, at].reshape(-1, ATT_DIM)
     old = lax.dot_general(q, keys_c, nt, preferred_element_type=F32)
-    new = lax.dot_general(q, keys_n, nt, preferred_element_type=F32) + bias_ref[...]
+    new = lax.dot_general(q, keys_n, nt, preferred_element_type=F32)
+    bias = bias_ref[...]
+    new = (new.reshape(together, tokens, -1) + bias[None]).reshape(together * tokens, -1)
     peak = jnp.maximum(
         jnp.max(old, axis=1, keepdims=True), jnp.max(new, axis=1, keepdims=True)
     )
@@ -157,9 +174,9 @@
     both = jnp.dot(old, vc_ref[k], preferred_element_type=F32) + jnp.dot(
         new, vn_ref[k], preferred_element_type=F32
     )
-    att_ref[:, lanes(h * ATT_DIM, ATT_DIM)] = (
-        both[:, :ATT_DIM] / both[:, ATT_DIM:]
-    ).astype(BF16)
+    result = (both[:, :ATT_DIM] / both[:, ATT_DIM:]).astype(BF16)
+    for e in range(together):
+        att_ref[:, own[e]] = result[e * tokens : (e + 1) * tokens]
 
 
 def comm_kernel(
@@ -321,8 +338,14 @@
     tokens = x_ref.shape[0]
     seen = iota((tokens, fresh), 1) <= me * tokens + iota((tokens, fresh), 0)
     bias_ref[...] = jnp.where(seen, 0.0, NEG)
-    early = max(1, chunks // 2)
-    late = max(1, chunks - early)
+    pairs = width // 128
+    early = n2
+    ahead = pairs * 3 // 4
+
+    def pair(p, _):
+        within_pair(p, x_ref, run_ref, at_ref, gram_ref, part_ref)
+        return 0
+
 
     def forward(kind, d):
         src = allc_ref if kind == 0 else alln_ref
@@ -389,17 +412,10 @@
         )
 
     def first_part(j, _):
-        pairs = width // 128
-
-        def pair(p, _):
-            within_pair(p, x_ref, run_ref, at_ref, gram_ref, part_ref)
-            return 0
-
-        lax.fori_loop(j * pairs // early, (j + 1) * pairs // early, pair, 0)
-        combine(j, 0)
+        lax.fori_loop(j * ahead // early, (j + 1) * ahead // early, pair, 0)
         for d in range(1, n2):
 
-            @pl.when(j == (d * early) // n2)
+            @pl.when(j == d)
             def _():
                 remote_slot(0, d).wait_recv()
                 forward(0, d).start()
@@ -435,22 +451,23 @@
             ext_ref[k, :, :ATT_DIM] = all_ref[:, :, at : at + ATT_DIM].reshape(-1, ATT_DIM)
             ext_ref[k, :, ATT_DIM:] = jnp.ones((ext_ref.shape[1], ATT_DIM), BF16)
 
+    q_heads = q_ref.shape[1] // ATT_DIM
+    steps = q_heads // 2 if (q_heads // kv_here) % 2 == 0 else q_heads
+
+    def head(h, _):
+        attend(h, q_ref, allc_ref, alln_ref, bias_ref, vc_ref, vn_ref, att_ref)
+        return 0
+
     def second_part(j, _):
-        q_heads = q_ref.shape[1] // ATT_DIM
-
-        def head(h, _):
-            attend(h, q_ref, allc_ref, alln_ref, bias_ref, vc_ref, vn_ref, att_ref)
-            return 0
-
-        lax.fori_loop(j * q_heads // late, (j + 1) * q_heads // late, head, 0)
-
-        @pl.when(early + j < chunks)
-        def _():
-            combine(early + j, 0)
-
+        rest = pairs - ahead
+        lax.fori_loop(
+            ahead + j * rest // chunks, ahead + (j + 1) * rest // chunks, pair, 0
+        )
+        lax.fori_loop(j * steps // chunks, (j + 1) * steps // chunks, head, 0)
+        combine(j, 0)
         return 0
 
-    lax.fori_loop(0, late, second_part, 0)
+    lax.fori_loop(0, chunks, second_part, 0)
 
     def drain(j, _):
         back_copy(j, 1 - i).wait_recv()
@@ -494,7 +511,7 @@
 
 def final_kernel(
     part_ref,
-    run_ref,
+    fade_ref,
     sout_ref,
     state_ref,
     meta_ref,
@@ -504,7 +521,7 @@
     scale_ref,
 ):
     tokens, width = part_ref.shape
-    heads = run_ref.shape[1]
+    heads = fade_ref.shape[1]
     per_group = min(SSM_HEADS // GROUPS, heads)
     z = lax.axis_index("head")
     group0 = z * heads // (SSM_HEADS // GROUPS)
@@ -514,7 +531,7 @@
     scale = (magnitude + 1e-6) / 127.0
     scale_ref[...] = scale
     code_ref[...] = (nk_ref[...].astype(F32) / scale).astype(BF16)
-    fade = jnp.exp2(run_ref[:tokens]).astype(BF16)
+    fade = fade_ref[...]
     for b in range(width // block):
         here = pl.ds(b * block, block)
         g = group0 + (b * block) // (per_group * HEAD_DIM)
@@ -554,11 +571,12 @@
     groups_here = heads // per_group
     limit = pltpu.CompilerParams(vmem_limit_bytes=60 * 1024 * 1024)
     shape = jax.ShapeDtypeStruct
-    state, run, at, gram, meta, kvc, kvn = pl.pallas_call(
+    state, run, fade, at, gram, meta, kvc, kvn = pl.pallas_call(
         local_kernel,
         out_shape=(
             shape((STATE, width), BF16),
-            shape((tokens + 8, heads), F32),
+            shape((tokens + 16, 3 * heads), BF16),
+            shape((tokens, heads), BF16),
             shape((heads, tokens), F32),
             shape((groups_here, tokens, tokens), F32),
             shape((1, width + channels), F32),
@@ -566,7 +584,7 @@
             shape((tokens, 2 * kvw), BF16),
         ),
         in_specs=[VMEM] * 13,
-        out_specs=(VMEM,) * 7,
+        out_specs=(VMEM,) * 8,
         compiler_params=limit,
         name="local",
     )(
@@ -641,7 +659,7 @@
         out_specs=(VMEM,) * 3,
         compiler_params=limit,
         name="finish",
-    )(part, run, state_out, carried, allm, new_keys)
+    )(part, fade, state_out, carried, allm, new_keys)
     return (y, attended, codes, scale.reshape(channels))
 
 

time: 92.3 us -> 76.8 us (0.83)
  Pallas kernels: 90.6 us -> 75.1 us
    pallas_call x1, Pallas kernels: 79.1 us -> 63.5 us  [body(): pl.pallas_call(functools.partial(comm_kernel, n, chunks), out_shape=(shap...]
where the time goes in v2:
time: 76.8 us; the launch traced here: 76.6 us
  Pallas kernels  75.1 us (98%)
  local copies, waits for them, and re-layouts  0.88 us (1%)
    pallas_call x1, Pallas kernels, body(): pl.pallas_call(functools.partial(comm_kernel, n, chunks), out_shape=(shap...  63.5 us
    pallas_call x1, Pallas kernels, body(): pl.pallas_call(local_kernel, out_shape=(shape((STATE, width), BF16), shap...  6.76 us
    pallas_call x1, Pallas kernels, body(): pl.pallas_call(final_kernel, out_shape=(shape((tokens, width), BF16), sha...  4.8 us

profile of v2, /device:TPU:29, one launch (start us, length us, event | category | flops | bytes accessed | tf_op | source)
XLA Modules:
  0.0 76.6 jit_solution(2838290630261049441)
XLA Ops:
  0.6 6.8 %local.1 = (bf16[256,4096]{1,0:T(8,128)(2,1)}, bf16[208,192]{1,0:T(8,128)(2,1)}, bf16[192,64]{1,0:T(8,128)(2,1)}, f32[64,192]{1,0:T(8,128)}, f32[2,192,192]{2,1,...) custom-call(bf16[192,4096]{1,0:T(8,128)(2,1)} %x_ref.3, ...), custom_call_target="tpu_custom_call" | custom-call | tf_op jit(solution)/shard_map/local/pallas_call | solution.py:574
  7.4 63.5 %exchange.1 = (bf16[256,4096]{1,0:T(8,128)(2,1)}, f32[8,1,5120]{2,1,0:T(1,128)}, bf16[192,4096]{1,0:T(8,128)(2,1)}, bf16[192,2048]{1,0:T(8,128)(2,1)}) custom-call(bf16[256,4096]{1,0:T(8,128)(2,1)} %get-tuple-element.19.state_ref, bf16[128,512]{1,0:T(8,128)(2,1)} %get-tuple-element.20.kvc_ref, bf16[192,512]{1,0:T(8,128)(2,1)} %get-tuple-element.21.kvn_ref, ...), custom_call_target="tpu_custom_call" | custom-call | tf_op jit(solution)/shard_map/exchange/pallas_call | solution.py:612
  70.9 0.0 copy-start
  70.9 4.8 %finish.1 = (bf16[192,4096]{1,0:T(8,128)(2,1)}, bf16[192,1024]{1,0:T(8,128)(2,1)}, f32[1,1024]{1,0:T(1,128)}) custom-call(bf16[192,4096]{1,0:T(8,128)(2,1)} %get-tuple-element.26.part_ref, bf16[192,64]{1,0:T(8,128)(2,1)} %get-tuple-element.27.fade_ref, bf16[192,2048]{1,0:T(8,128)(2,1)} %sout_ref.3, bf16[256,4096]{1,0:T(8,128)(2,1)} %get-tuple-element.28.state_ref, ...), custom_call_target="tpu_custom_call" | custom-call | tf_op jit(solution)/shard_map/finish/pallas_call | solution.py:651
  75.7 0.0 copy-done
  75.7 0.9 %copy.19 = bf16[192,2048]{1,0:T(8,128)(2,1)} copy(bf16[192,2048]{1,0:T(8,128)(2,1)S(1)} %copy-done) | data formatting | bytes 1572864
Async XLA Ops:
  70.9 4.8 %copy-start = (bf16[192,2048]{1,0:T(8,128)(2,1)S(1)}, bf16[192,2048]{1,0:T(8,128)(2,1)}, u32[]{:S(2)}) copy-start(bf16[192,2048]{1,0:T(8,128)(2,1)} %get-tuple-element.39) | copy-start | bytes 2359300

commit v3 on v2

--- a/solution.py
+++ b/solution.py
@@ -338,12 +338,14 @@
     tokens = x_ref.shape[0]
     seen = iota((tokens, fresh), 1) <= me * tokens + iota((tokens, fresh), 0)
     bias_ref[...] = jnp.where(seen, 0.0, NEG)
-    pairs = width // 128
+    twin = 2 if width % 256 == 0 else 1
+    pairs = width // 128 // twin
     early = n2
     ahead = pairs * 3 // 4
 
     def pair(p, _):
-        within_pair(p, x_ref, run_ref, at_ref, gram_ref, part_ref)
+        for e in range(twin):
+            within_pair(twin * p + e, x_ref, run_ref, at_ref, gram_ref, part_ref)
         return 0
 
 
@@ -454,6 +456,8 @@
     q_heads = q_ref.shape[1] // ATT_DIM
     steps = q_heads // 2 if (q_heads // kv_here) % 2 == 0 else q_heads
 
+    served = steps * 3 // 4
+
     def head(h, _):
         attend(h, q_ref, allc_ref, alln_ref, bias_ref, vc_ref, vn_ref, att_ref)
         return 0
@@ -463,11 +467,12 @@
         lax.fori_loop(
             ahead + j * rest // chunks, ahead + (j + 1) * rest // chunks, pair, 0
         )
-        lax.fori_loop(j * steps // chunks, (j + 1) * steps // chunks, head, 0)
+        lax.fori_loop(j * served // chunks, (j + 1) * served // chunks, head, 0)
         combine(j, 0)
         return 0
 
     lax.fori_loop(0, chunks, second_part, 0)
+    lax.fori_loop(served, steps, head, 0)
 
     def drain(j, _):
         back_copy(j, 1 - i).wait_recv()

time: 76.8 us -> 78.7 us (1.025)
  the two profiles are of different devices: /device:TPU:29 before, /device:TPU:28 now
where the time goes in v3:
time: 78.7 us; the launch traced here: 78.6 us
  Pallas kernels  77 us (98%)
  local copies, waits for them, and re-layouts  0.88 us (1%)
    pallas_call x1, Pallas kernels, body(): pl.pallas_call(functools.partial(comm_kernel, n, chunks), out_shape=(shap...  65.5 us
    pallas_call x1, Pallas kernels, body(): pl.pallas_call(local_kernel, out_shape=(shape((STATE, width), BF16), shap...  6.75 us
    pallas_call x1, Pallas kernels, body(): pl.pallas_call(final_kernel, out_shape=(shape((tokens, width), BF16), sha...  4.78 us

profile of v3, /device:TPU:28, one launch (start us, length us, event | category | flops | bytes accessed | tf_op | source)
XLA Modules:
  0.0 78.6 jit_solution(9663159185381215285)
XLA Ops:
  0.6 6.7 %local.1 = (bf16[256,4096]{1,0:T(8,128)(2,1)}, bf16[208,192]{1,0:T(8,128)(2,1)}, bf16[192,64]{1,0:T(8,128)(2,1)}, f32[64,192]{1,0:T(8,128)}, f32[2,192,192]{2,1,...) custom-call(bf16[192,4096]{1,0:T(8,128)(2,1)} %x_ref.3, ...), custom_call_target="tpu_custom_call" | custom-call | tf_op jit(solution)/shard_map/local/pallas_call | solution.py:579
  7.4 65.5 %exchange.1 = (bf16[256,4096]{1,0:T(8,128)(2,1)}, f32[8,1,5120]{2,1,0:T(1,128)}, bf16[192,4096]{1,0:T(8,128)(2,1)}, bf16[192,2048]{1,0:T(8,128)(2,1)}) custom-call(bf16[256,4096]{1,0:T(8,128)(2,1)} %get-tuple-element.19.state_ref, bf16[128,512]{1,0:T(8,128)(2,1)} %get-tuple-element.20.kvc_ref, bf16[192,512]{1,0:T(8,128)(2,1)} %get-tuple-element.21.kvn_ref, ...), custom_call_target="tpu_custom_call" | custom-call | tf_op jit(solution)/shard_map/exchange/pallas_call | solution.py:617
  72.9 0.0 copy-start
  72.9 4.8 %finish.1 = (bf16[192,4096]{1,0:T(8,128)(2,1)}, bf16[192,1024]{1,0:T(8,128)(2,1)}, f32[1,1024]{1,0:T(1,128)}) custom-call(bf16[192,4096]{1,0:T(8,128)(2,1)} %get-tuple-element.26.part_ref, bf16[192,64]{1,0:T(8,128)(2,1)} %get-tuple-element.27.fade_ref, bf16[192,2048]{1,0:T(8,128)(2,1)} %sout_ref.3, bf16[256,4096]{1,0:T(8,128)(2,1)} %get-tuple-element.28.state_ref, ...), custom_call_target="tpu_custom_call" | custom-call | tf_op jit(solution)/shard_map/finish/pallas_call | solution.py:656
  77.7 0.0 copy-done
  77.7 0.9 %copy.19 = bf16[192,2048]{1,0:T(8,128)(2,1)} copy(bf16[192,2048]{1,0:T(8,128)(2,1)S(1)} %copy-done) | data formatting | bytes 1572864
Async XLA Ops:
  72.9 4.8 %copy-start = (bf16[192,2048]{1,0:T(8,128)(2,1)S(1)}, bf16[192,2048]{1,0:T(8,128)(2,1)}, u32[]{:S(2)}) copy-start(bf16[192,2048]{1,0:T(8,128)(2,1)} %get-tuple-element.39) | copy-start | bytes 2359300

commit v4 on v3

--- a/solution.py
+++ b/solution.py
@@ -215,6 +215,7 @@
     pre_s,
     pre_r,
     rel_s,
+    mir_s,
     back_s,
     back_r,
 ):
@@ -315,6 +316,24 @@
             ((c + n2 - 1) % n2) * 2 + i,
         )
 
+    def mirror_copy(j):
+        return remote(
+            incl_ref.at[0, j],
+            recv_ref.at[0, j],
+            mir_s.at[j],
+            pre_r.at[0, j],
+            ((c + n2 - 1) % n2) * 2 + i,
+        )
+
+    def cross_copy(j):
+        return remote(
+            incl_ref.at[1, j],
+            recv_ref.at[1, j],
+            mir_s.at[j],
+            pre_r.at[1, j],
+            ((c + 2) % n2) * 2 + i,
+        )
+
     def logs(r, j):
         return allm_ref[r, :, lanes(i * half + j * size, size)]
 
@@ -330,6 +349,12 @@
         @pl.when(sends(0))
         def _():
             pre_copy(0, j, 0).start()
+
+        if levels >= 2:
+
+            @pl.when(c % 4 == 1)
+            def _():
+                mirror_copy(j).start()
 
         return 0
 
@@ -357,12 +382,24 @@
         )
 
     def combine(j, _):
+        if levels >= 2:
+
+            @pl.when(c % 4 == 0)
+            def _():
+                mirror_copy(j).wait_recv()
+                nxt = (c + 1) % n2
+                keep = jnp.exp2(logs(2 * nxt, j) + logs(2 * nxt + 1, j))
+                incl_ref[1, j] = (
+                    keep * incl_ref[0, j].astype(F32) + recv_ref[0, j].astype(F32)
+                ).astype(BF16)
+                cross_copy(j).start()
+
         for l in range(levels):
 
             @pl.when(c % (2 ** (l + 1)) >= 2**l)
             def _():
                 pre_copy(l, j, 0).wait_recv()
-                if l >= 1:
+                if l >= 2:
 
                     @pl.when(c % 2 == 1)
                     def _():
@@ -456,7 +493,7 @@
     q_heads = q_ref.shape[1] // ATT_DIM
     steps = q_heads // 2 if (q_heads // kv_here) % 2 == 0 else q_heads
 
-    served = steps * 3 // 4
+    served = steps * 7 // 8
 
     def head(h, _):
         attend(h, q_ref, allc_ref, alln_ref, bias_ref, vc_ref, vn_ref, att_ref)
@@ -485,11 +522,21 @@
                 for r in targets(l):
                     pre_copy(l, j, r).wait_send()
 
-            if l >= 1:
+            if l >= 2:
 
                 @pl.when((c % (2 ** (l + 1)) >= 2**l) & (c % 2 == 1))
                 def _():
                     relay_copy(l, j).wait_send()
+
+        if levels >= 2:
+
+            @pl.when(c % 4 == 1)
+            def _():
+                mirror_copy(j).wait_send()
+
+            @pl.when(c % 4 == 0)
+            def _():
+                cross_copy(j).wait_send()
 
         return 0
 
@@ -647,6 +694,7 @@
             dma((levels, chunks)),
             dma((chunks,)),
             dma((chunks,)),
+            dma((chunks,)),
         ],
         compiler_params=pltpu.CompilerParams(
             collective_id=0, has_side_effects=True, vmem_limit_bytes=60 * 1024 * 1024

time: 78.7 us -> 70 us (0.89)
  the two profiles are of different devices: /device:TPU:28 before, /device:TPU:29 now
where the time goes in v4:
time: 70 us; the launch traced here: 69.2 us
  Pallas kernels  67.6 us (97%)
  local copies, waits for them, and re-layouts  0.88 us (1%)
    pallas_call x1, Pallas kernels, body(): pl.pallas_call(functools.partial(comm_kernel, n, chunks), out_shape=(shap...  56.1 us
    pallas_call x1, Pallas kernels, body(): pl.pallas_call(local_kernel, out_shape=(shape((STATE, width), BF16), shap...  6.76 us
    pallas_call x1, Pallas kernels, body(): pl.pallas_call(final_kernel, out_shape=(shape((tokens, width), BF16), sha...  4.8 us

profile of v4, /device:TPU:29, one launch (start us, length us, event | category | flops | bytes accessed | tf_op | source)
XLA Modules:
  0.0 69.2 jit_solution(5387337597381664387)
XLA Ops:
  0.6 6.8 %local.1 = (bf16[256,4096]{1,0:T(8,128)(2,1)}, bf16[208,192]{1,0:T(8,128)(2,1)}, bf16[192,64]{1,0:T(8,128)(2,1)}, f32[64,192]{1,0:T(8,128)}, f32[2,192,192]{2,1,...) custom-call(bf16[192,4096]{1,0:T(8,128)(2,1)} %x_ref.3, ...), custom_call_target="tpu_custom_call" | custom-call | tf_op jit(solution)/shard_map/local/pallas_call | solution.py:626
  7.4 56.1 %exchange.1 = (bf16[256,4096]{1,0:T(8,128)(2,1)}, f32[8,1,5120]{2,1,0:T(1,128)}, bf16[192,4096]{1,0:T(8,128)(2,1)}, bf16[192,2048]{1,0:T(8,128)(2,1)}) custom-call(bf16[256,4096]{1,0:T(8,128)(2,1)} %get-tuple-element.19.state_ref, bf16[128,512]{1,0:T(8,128)(2,1)} %get-tuple-element.20.kvc_ref, bf16[192,512]{1,0:T(8,128)(2,1)} %get-tuple-element.21.kvn_ref, ...), custom_call_target="tpu_custom_call" | custom-call | tf_op jit(solution)/shard_map/exchange/pallas_call | solution.py:664
  63.5 0.0 copy-start
  63.5 4.8 %finish.1 = (bf16[192,4096]{1,0:T(8,128)(2,1)}, bf16[192,1024]{1,0:T(8,128)(2,1)}, f32[1,1024]{1,0:T(1,128)}) custom-call(bf16[192,4096]{1,0:T(8,128)(2,1)} %get-tuple-element.26.part_ref, bf16[192,64]{1,0:T(8,128)(2,1)} %get-tuple-element.27.fade_ref, bf16[192,2048]{1,0:T(8,128)(2,1)} %sout_ref.3, bf16[256,4096]{1,0:T(8,128)(2,1)} %get-tuple-element.28.state_ref, ...), custom_call_target="tpu_custom_call" | custom-call | tf_op jit(solution)/shard_map/finish/pallas_call | solution.py:704
  68.3 0.0 copy-done
  68.3 0.9 %copy.19 = bf16[192,2048]{1,0:T(8,128)(2,1)} copy(bf16[192,2048]{1,0:T(8,128)(2,1)S(1)} %copy-done) | data formatting | bytes 1572864
Async XLA Ops:
  63.5 4.8 %copy-start = (bf16[192,2048]{1,0:T(8,128)(2,1)S(1)}, bf16[192,2048]{1,0:T(8,128)(2,1)}, u32[]{:S(2)}) copy-start(bf16[192,2048]{1,0:T(8,128)(2,1)} %get-tuple-element.39) | copy-start | bytes 2359300
